TPU v7x, 32 devices: a whole 2x2x4 slice. The times are simulated.
32 devices in a mesh: alpha: 8 (over y, x, core), beta: 4 (over z).
Axes of the slice: x: 2, y: 2, z: 4, core: 2. Of those that a mesh axis runs over, the one named last changes fastest.
Arguments:
- coefficients: bfloat16 [4096, 4096], P('alpha', 'beta'), may hold values from -6 to 6
- couplings: bfloat16 [8, 256, 256], replicated, may hold values from -0.375 to 0.375
- exc_list: int32 [8, 8, 3], replicated, may hold values from 0 to 15, as said below
- counts: int32 [8, 8], replicated, may hold values from 0 to 1, as said below
- beta_tiles: bfloat16 [4, 1024, 4096], P(None, None, 'beta'), may hold values from -0.09375 to 0.09375
Outputs:
- sigma_vector: float32 [4096, 4096], P('alpha', 'beta')
Inputs may be any that keep to these rules, and one draw needn't show every extreme that they name: `exc_list`: entry [s, p] describes the slot from alpha device s to alpha device p: field 0 is a source block held by device s (from s * 2 to s * 2 + 1), field 1 a target block held by device p (from p * 2 to p * 2 + 1), field 2 a coupling index below 8. `counts`: 1 where a slot is live, 0 where it is empty; in every draw some device p has a live slot from every device s.
All inputs are finite; a program needn't handle non-finite values.
Results may differ from a plain program's by a relative error of at most 0.0029.
Values may be sent and summed in bfloat16 or wider, within the bound.
A program may use at most 192 MiB of HBM per device.

v0:
```python
import functools

import jax
import jax.numpy as jnp
from jax import lax
from jax.experimental import pallas as pl
from jax.experimental.pallas import tpu as pltpu
from jax.sharding import PartitionSpec as P

MESH = pl.DeviceIdType.MESH
WIDTHS = (1, 2, 2, 2, 1)
TILE = 256
AHEAD = 1


def split(columns):
    unit = columns // sum(WIDTHS)
    widths = [unit * part for part in WIDTHS]
    return widths, [sum(widths[:c]) for c in range(len(widths))]


def flip(position, mask):
    bit = lax.rem(lax.div(position, mask), 2)
    return position + mask * (1 - 2 * bit)


def kernel(
    n_alpha, n_beta, rounds, chunks,
    exc_ref, counts_ref, coupling_ref, c_hbm, b_hbm, out_ref,
    weights, gathered, tiles, held, moved,
    send_sem, recv_sem, own_sem, zsend_sem, zrecv_sem, tile_sem,
):
    n_chips = n_alpha // 2
    n_blocks, order = c_hbm.shape[0], c_hbm.shape[1]
    n_stops = b_hbm.shape[0]
    widths, starts = split(out_ref.shape[1])
    alpha, beta = lax.axis_index("alpha"), lax.axis_index("beta")
    chip, core = lax.div(alpha, 2), lax.rem(alpha, 2)

    def mask_of(step, which):
        return (1 - which) * 2**step + which * 2 ** (rounds - 1 - step)

    def origin(label, which):
        source = chip
        for step in range(rounds):
            if (label >> step) & 1:
                source = flip(source, mask_of(step, which))
        return source * 2 + which

    if n_beta == n_stops:
        way, far, near = 1 - 2 * core, n_beta // 2, n_beta - 1 - n_beta // 2
    else:
        way, far, near = 1, n_stops - 1, 0
    ahead = lax.rem(beta + way + n_beta, n_beta)
    behind = lax.rem(beta - way + n_beta, n_beta)

    sibling = (alpha + 1 - 2 * core, beta)
    neighbours = [(flip(chip, mask_of(step, core)) * 2 + core, beta) for step in range(rounds)]
    greeted = neighbours + [sibling, (alpha, ahead), (alpha, behind)]
    barrier = pltpu.get_barrier_semaphore()
    for device in greeted:
        pl.semaphore_signal(barrier, inc=1, device_id=device, device_id_type=MESH)
    own = []
    for c in range(chunks):
        own.append(
            pltpu.make_async_copy(c_hbm.at[:, :, pl.ds(starts[c], widths[c])], held[c].at[0], own_sem.at[c])
        )
    own[0].start()
    pl.semaphore_wait(barrier, len(greeted))

    def to_alpha(c, label, target, device):
        source = c_hbm.at[:, :, pl.ds(starts[c], widths[c])] if label == 0 else held[c].at[label]
        return pltpu.make_async_remote_copy(
            src_ref=source,
            dst_ref=held[c].at[target],
            send_sem=send_sem.at[c, target],
            recv_sem=recv_sem.at[c, target],
            device_id=device,
            device_id_type=MESH,
        )

    copies = [{} for _ in range(chunks)]

    def pass_on(c, label):
        for step in range(label.bit_length(), rounds):
            target = label + 2**step
            copies[c][target] = to_alpha(c, label, target, neighbours[step])
            copies[c][target].start()
        target = n_chips + label
        copies[c][target] = to_alpha(c, label, target, sibling)
        copies[c][target].start()

    def slot_of(hop):
        return lax.rem(hop * way + n_beta * n_stops, n_beta)

    hops = [{} for _ in range(chunks)]

    def to_beta(c, kind, hop):
        sign, device, index = (1, ahead, hop - 1) if kind == "far" else (-1, behind, far + hop - 1)
        copy = pltpu.make_async_remote_copy(
            src_ref=moved[c].at[slot_of(sign * (hop - 1))],
            dst_ref=moved[c].at[slot_of(sign * hop)],
            send_sem=zsend_sem.at[c, index],
            recv_sem=zrecv_sem.at[c, index],
            device_id=(alpha, device),
            device_id_type=MESH,
        )
        hops[c][kind, hop] = copy
        copy.start()

    for c in range(min(AHEAD, chunks)):
        if c > 0:
            own[c].start()
        pass_on(c, 0)
    tile_copy = pltpu.make_async_copy(b_hbm, tiles, tile_sem)
    tile_copy.start()

    sources = [origin(label, core) for label in range(n_chips)]
    sources += [origin(label, 1 - core) for label in range(n_chips)]
    picked = []
    for slot, source in enumerate(sources):
        live = counts_ref[source, alpha] == 1
        picked.append(jnp.clip(exc_ref[0, source, alpha] - source * n_blocks, 0, n_blocks - 1))
        target = exc_ref[1, source, alpha] - alpha * n_blocks
        matrix = coupling_ref[exc_ref[2, source, alpha]]
        for block in range(n_blocks):
            keep = jnp.where(live & (target == block), 1.0, 0.0).astype(jnp.float32)
            weights[pl.ds(block * order, order), pl.ds(slot * order, order)] = (
                matrix.astype(jnp.float32) * keep
            ).astype(jnp.bfloat16)

    def product(c):
        @pl.loop(0, out_ref.shape[1] // TILE)
        def _(n):
            columns = pl.ds(pl.multiple_of(n * TILE, TILE), TILE)
            left = jnp.concatenate([moved[c][d] for d in range(n_stops)], axis=1)
            right = jnp.concatenate(
                [tiles[d, pl.ds(starts[c], widths[c]), columns] for d in range(n_stops)], axis=0
            )
            value = jnp.dot(left, right, preferred_element_type=jnp.float32)
            if c == 0:
                out_ref[:, columns] = value
            else:
                out_ref[:, columns] += value

    def relay(c):
        for kind, last in (("far", far), ("near", near)):
            for hop in range(1, last):
                hops[c][kind, hop].wait_recv()
                to_beta(c, kind, hop + 1)

    def finish(c):
        for kind, last in (("far", far), ("near", near)):
            if last > 0:
                hops[c][kind, last].wait_recv()
        if c == 0:
            tile_copy.wait()
        product(c)

    for c in range(chunks):
        for label in range(1, n_chips):
            copies[c][label].wait_recv()
            pass_on(c, label)
            if label == 1 and c + AHEAD < chunks:
                own[c + AHEAD].start()
                pass_on(c + AHEAD, 0)
        own[c].wait()
        for label in range(n_chips):
            copies[c][n_chips + label].wait_recv()
        for slot in range(n_alpha):
            gathered[pl.ds(slot * order, order), pl.ds(0, widths[c])] = held[c][slot, picked[slot]]
        moved[c][0] = jnp.dot(
            weights[...], gathered[:, pl.ds(0, widths[c])], preferred_element_type=jnp.float32
        ).astype(jnp.bfloat16)
        to_beta(c, "far", 1)
        if near > 0:
            to_beta(c, "near", 1)
        if c >= 1:
            relay(c - 1)
        if c >= 2:
            finish(c - 2)
    relay(chunks - 1)
    for c in range(max(chunks - 2, 0), chunks):
        finish(c)
    for c in range(chunks):
        for copy in copies[c].values():
            copy.wait_send()
        for copy in hops[c].values():
            copy.wait_send()


def solution(mesh):
    n_alpha, n_beta = mesh.shape["alpha"], mesh.shape["beta"]
    n_chips = n_alpha // 2
    rounds = n_chips.bit_length() - 1

    def per_device(coefficients, couplings, exc_list, counts, beta_tiles):
        order = couplings.shape[1]
        rows, columns = coefficients.shape
        n_blocks = rows // order
        n_stops = beta_tiles.shape[0]
        widths, _ = split(columns)
        chunks = len(widths)
        vmem, smem = pl.BlockSpec(memory_space=pltpu.VMEM), pl.BlockSpec(memory_space=pltpu.SMEM)
        hbm = pl.BlockSpec(memory_space=pl.ANY)
        return pl.pallas_call(
            functools.partial(kernel, n_alpha, n_beta, rounds, chunks),
            out_shape=pltpu.VMEM((rows, columns), jnp.float32),
            in_specs=[smem, smem, vmem, hbm, hbm],
            out_specs=vmem,
            scratch_shapes=[
                pltpu.VMEM((rows, n_alpha * order), jnp.bfloat16),
                pltpu.VMEM((n_alpha * order, max(widths)), jnp.bfloat16),
                pltpu.VMEM(beta_tiles.shape, jnp.bfloat16),
                [pltpu.VMEM((n_alpha, n_blocks, order, width), jnp.bfloat16) for width in widths],
                [pltpu.VMEM((n_stops, rows, width), jnp.bfloat16) for width in widths],
                pltpu.SemaphoreType.DMA((chunks, n_alpha)),
                pltpu.SemaphoreType.DMA((chunks, n_alpha)),
                pltpu.SemaphoreType.DMA((chunks,)),
                pltpu.SemaphoreType.DMA((chunks, n_stops - 1)),
                pltpu.SemaphoreType.DMA((chunks, n_stops - 1)),
                pltpu.SemaphoreType.DMA(()),
            ],
            compiler_params=pltpu.CompilerParams(
                collective_id=0, has_side_effects=True, vmem_limit_bytes=48 * 2**20
            ),
        )(
            exc_list.transpose(2, 0, 1),
            counts,
            couplings,
            coefficients.reshape(n_blocks, order, columns),
            beta_tiles,
        )

    placed = (P("alpha", "beta"), P(), P(), P(), P(None, None, "beta"))
    return jax.shard_map(
        per_device, mesh=mesh, in_specs=placed, out_specs=P("alpha", "beta"), check_vma=False
    )
```

profile of v0, /device:TPU:0, one launch (start us, length us, event | category | flops | bytes accessed | tf_op | source)
XLA Modules:
  0.0 98.3 jit_solution(10617737470537366432)
XLA Ops:
  0.0 0.0 copy-start
  0.0 1.2 %copy-done = bf16[8,256,256]{2,1,0:T(8,128)(2,1)S(1)} copy-done((bf16[8,256,256]{2,1,0:T(8,128)(2,1)S(1)}, bf16[8,256,256]{2,1,0:T(8,128)(2,1)}, u32[]{:S(2)}) %copy-start) | copy-done | bytes 1048600
  1.2 0.0 copy-start.1
  1.2 1.2 %copy-done.1 = bf16[512,1024]{1,0:T(8,128)(2,1)S(1)} copy-done((bf16[512,1024]{1,0:T(8,128)(2,1)S(1)}, bf16[512,1024]{1,0:T(8,128)(2,1)}, u32[]{:S(2)}) %copy-start.1) | copy-done | bytes 1048600
  2.5 0.0 copy-start.2
  2.5 0.7 copy-done.2
  3.2 0.0 copy-start.3
  3.2 0.7 copy-done.3
  3.8 93.1 %shard_map.55 = f32[512,1024]{1,0:T(8,128)S(1)} custom-call(s32[3,8,8]{2,1,0:T(8,128)S(1)} %bitcast.3, s32[8,8]{1,0:T(8,128)S(1)} %copy-done.3, bf16[8,256,256]{2,1,0:T(8,128)(2,1)S(1)} %copy-done, bf16[2,256,1024]{2,1,0:T(8,128)(2,1)S(1)} %bitcast.2, bf16[4,1024,1024]{2,1,0:T(8,128)(2,1)} %b_hbm.1), custom_call_target="tpu_custom_call" | custom-call | tf_op jit(solution)/shard_map/pallas_call | solution.py:206
  97.0 1.3 %copy.7 = f32[512,1024]{1,0:T(8,128)} copy(f32[512,1024]{1,0:T(8,128)S(1)} %shard_map.55) | data formatting | bytes 4194304
Async XLA Ops:
  0.0 1.2 %copy-start = (bf16[8,256,256]{2,1,0:T(8,128)(2,1)S(1)}, bf16[8,256,256]{2,1,0:T(8,128)(2,1)}, u32[]{:S(2)}) copy-start(bf16[8,256,256]{2,1,0:T(8,128)(2,1)} %coupling_ref.1) | copy-start | bytes 3145732
  1.2 1.2 %copy-start.1 = (bf16[512,1024]{1,0:T(8,128)(2,1)S(1)}, bf16[512,1024]{1,0:T(8,128)(2,1)}, u32[]{:S(2)}) copy-start(bf16[512,1024]{1,0:T(8,128)(2,1)} %param.5) | copy-start | bytes 3145732
  2.5 0.7 copy-start.2
  3.2 0.7 copy-start.3
where the time goes:
time: 98.6 us; the launch traced here: 98.3 us
  Pallas kernels  93.1 us (94%)
  local copies, waits for them, and re-layouts  5.16 us (5%)
    pallas_call x1, Pallas kernels, per_device(): pl.pallas_call(functools.partial(kernel, n_alpha, n_beta, rounds, chunks)...  93.1 us
    unnamed x9, local copies, waits for them, and re-layouts  5.16 us

commit v1 on v0

--- a/solution.py
+++ b/solution.py
@@ -11,6 +11,9 @@
 WIDTHS = (1, 2, 2, 2, 1)
 TILE = 256
 AHEAD = 1
+SHARES = (4, 4, 4, 2, 2)
+PIECES = 4
+LANES = 128
 
 
 def split(columns):
@@ -189,6 +192,320 @@
             copy.wait_send()
 
 
+def line_kernel(
+    n_alpha, n_beta, rounds, heights, early,
+    exc_hbm, counts_hbm, coupling_hbm, c_hbm, b_hbm, out_ref,
+    exc_ref, counts_ref, coupling_ref, weights, tiles, blocks, outer_tiles, partial, remote_sum, held, gathered,
+    in_sem, raw_send, raw_recv, sum_send, sum_recv, tile_send, tile_recv, spread_send, spread_recv, send_sem, recv_sem,
+):
+    n_chips = n_alpha // 2
+    n_blocks, order, columns = c_hbm.shape
+    chunks = len(heights)
+    offsets = [sum(heights[:c]) for c in range(chunks)]
+    alpha, beta = lax.axis_index("alpha"), lax.axis_index("beta")
+    chip, core = lax.div(alpha, 2), lax.rem(alpha, 2)
+    side = lax.div(beta, 2)
+    outer, inner = 3 * side, 1 + side
+    across, beyond = 2 - side, 3 - 3 * side
+    is_outer = beta == outer
+
+    def mask_of(step, which):
+        return (1 - which) * 2**step + which * 2 ** (rounds - 1 - step)
+
+    def origin(label, which):
+        source = chip
+        for step in range(rounds):
+            if (label >> step) & 1:
+                source = flip(source, mask_of(step, which))
+        return source * 2 + which
+
+    def distance(source):
+        return lax.rem(beta - source + n_beta, n_beta)
+
+    sources = [origin(label, core) for label in range(n_chips)]
+    sources += [origin(label, 1 - core) for label in range(n_chips)]
+    sibling = (alpha + 1 - 2 * core, beta)
+    neighbours = [(flip(chip, mask_of(step, core)) * 2 + core, beta) for step in range(rounds)]
+    near = (alpha, is_outer.astype(jnp.int32) * inner + (1 - is_outer.astype(jnp.int32)) * outer)
+    facing = (alpha, across)
+
+    barrier = pltpu.get_barrier_semaphore()
+    for device in neighbours + [sibling, near]:
+        pl.semaphore_signal(barrier, inc=1, device_id=device, device_id_type=MESH)
+
+    @pl.when(jnp.logical_not(is_outer))
+    def _():
+        pl.semaphore_signal(barrier, inc=1, device_id=facing, device_id_type=MESH)
+
+    local = [
+        pltpu.make_async_copy(exc_hbm, exc_ref, in_sem.at[0]),
+        pltpu.make_async_copy(counts_hbm, counts_ref, in_sem.at[1]),
+        pltpu.make_async_copy(coupling_hbm, coupling_ref, in_sem.at[2]),
+        pltpu.make_async_copy(c_hbm, blocks.at[beta], in_sem.at[3]),
+        pltpu.make_async_copy(b_hbm, tiles, in_sem.at[4]),
+    ]
+    for copy in local:
+        copy.start()
+    pl.semaphore_wait(barrier, rounds + 3 - is_outer.astype(jnp.int32))
+
+    def rows_of(c):
+        return pl.ds(offsets[c], heights[c])
+
+    def remote(source, target, send, recv, device):
+        return pltpu.make_async_remote_copy(
+            src_ref=source, dst_ref=target, send_sem=send, recv_sem=recv, device_id=device, device_id_type=MESH
+        )
+
+    def raw(c, plane, kind, device):
+        source = c_hbm.at[:, rows_of(c)] if kind < 2 else blocks.at[plane, :, rows_of(c)]
+        return remote(
+            source, blocks.at[plane, :, rows_of(c)], raw_send.at[kind, c], raw_recv.at[plane, c], device
+        )
+
+    def sum_copy(c):
+        here = remote_sum.at[:, rows_of(c)]
+        return remote(here, here, sum_send.at[c], sum_recv.at[c], near)
+
+    piece = 2 * b_hbm.shape[1] // n_alpha
+    part = piece // PIECES
+
+    def tile_copy(q):
+        row = alpha * piece + q * part
+        which = lax.div(row, b_hbm.shape[1])
+        tile = (1 - which) * 2 + which * (1 + 2 * side)
+        source = b_hbm.at[tile, pl.ds(pl.multiple_of(lax.rem(row, b_hbm.shape[1]), part), part)]
+        target = outer_tiles.at[pl.ds(pl.multiple_of(row, part), part)]
+        return remote(source, target, tile_send.at[q], tile_recv.at[q], near)
+
+    def tile_spread(q, label, target, device):
+        here = outer_tiles.at[pl.ds(pl.multiple_of(sources[label] * piece + q * part, part), part)]
+        return remote(here, here, spread_send.at[q, target], spread_recv.at[q, target], device)
+
+    def held_spread(c, label, target, device):
+        return remote(held[c].at[label], held[c].at[target], send_sem.at[c, target], recv_sem.at[c, target], device)
+
+    def spread(make, index, label, sent):
+        for step in range(label.bit_length(), rounds):
+            sent.append(make(index, label, label + 2**step, neighbours[step]))
+            sent[-1].start()
+        sent.append(make(index, label, n_chips + label, sibling))
+        sent[-1].start()
+
+    def arrive(make, index, label):
+        make(index, label, label, sibling).wait_recv()
+
+    def tile_arrive(q, label):
+        here = outer_tiles.at[pl.ds(pl.multiple_of(sources[label] * piece + q * part, part), part)]
+        remote(here, here, spread_send.at[q, label], spread_recv.at[q, label], sibling).wait_recv()
+
+    def set_weights():
+        for copy in local[:3]:
+            copy.wait()
+        picked = []
+        for slot, source in enumerate(sources):
+            live = counts_ref[source, alpha] == 1
+            picked.append(jnp.clip(exc_ref[0, source, alpha] - source * n_blocks, 0, n_blocks - 1))
+            target = exc_ref[1, source, alpha] - alpha * n_blocks
+            matrix = coupling_ref[exc_ref[2, source, alpha]]
+            for block in range(n_blocks):
+                keep = jnp.where(live & (target == block), 1.0, 0.0).astype(jnp.float32)
+                value = (matrix.astype(jnp.float32) * keep).astype(jnp.bfloat16)
+                for half in range(order // LANES):
+                    weights[half, pl.ds(block * order, order), pl.ds(slot * LANES, LANES)] = value[
+                        :, half * LANES : (half + 1) * LANES
+                    ]
+        return picked
+
+    def product(c, terms, store):
+        @pl.loop(0, columns // TILE)
+        def _(n):
+            at = pl.ds(pl.multiple_of(n * TILE, TILE), TILE)
+            value = None
+            for plane, right in terms:
+                left = blocks[plane, :, rows_of(c)].reshape(n_blocks * heights[c], columns)
+                term = jnp.dot(left, right(at), preferred_element_type=jnp.float32)
+                value = term if value is None else value + term
+            store(at, value)
+
+    def own_tile(plane):
+        return lambda at: tiles[distance(plane), :, at]
+
+    def far_tile(k):
+        return lambda at: outer_tiles[pl.ds(k * columns, columns), at]
+
+    def store_held(c):
+        def store(at, value):
+            held[c][0, :, :, at] = value.astype(jnp.bfloat16).reshape(n_blocks, heights[c], TILE)
+        return store
+
+    def store_sum(c):
+        def store(at, value):
+            remote_sum[:, rows_of(c), at] = value.astype(jnp.bfloat16).reshape(n_blocks, heights[c], TILE)
+        return store
+
+    def store_partial(c):
+        def store(at, value):
+            partial[:, rows_of(c), at] = value.reshape(n_blocks, heights[c], TILE)
+        return store
+
+    def relay(c, label):
+        arrive(held_spread, c, label)
+        spread(held_spread, c, label, sent)
+
+    def finish(c, picked):
+        for label in range(n_chips):
+            arrive(held_spread, c, n_chips + label)
+        half, within = offsets[c] // LANES, offsets[c] % LANES
+        for slot in range(n_alpha):
+            gathered[half, pl.ds(slot * LANES + within, heights[c])] = held[c][slot, picked[slot]]
+        if within + heights[c] == LANES:
+            @pl.loop(0, columns // TILE)
+            def _(n):
+                at = pl.ds(pl.multiple_of(n * TILE, TILE), TILE)
+                value = jnp.dot(weights[half], gathered[half, :, at], preferred_element_type=jnp.float32)
+                if half == 0:
+                    out_ref[:, at] = value
+                else:
+                    out_ref[:, at] += value
+
+    def follow(c, picked):
+        if c >= 1:
+            for label in range(1, n_chips):
+                relay(c - 1, label)
+        if c >= 2:
+            finish(c - 2, picked)
+
+    def end(picked):
+        for label in range(1, n_chips):
+            relay(chunks - 1, label)
+        for c in range(max(chunks - 2, 0), chunks):
+            finish(c, picked)
+        for copy in sent:
+            copy.wait_send()
+
+    sent = []
+
+    def start(copy):
+        sent.append(copy)
+        copy.start()
+
+    @pl.when(is_outer)
+    def _():
+        for q in range(PIECES):
+            start(tile_copy(q))
+        for c in range(chunks):
+            start(raw(c, outer, 0, near))
+        picked = set_weights()
+        local[3].wait()
+        local[4].wait()
+        for c in range(chunks):
+            raw(c, inner, 0, near).wait_recv()
+            product(c, [(outer, own_tile(outer)), (inner, own_tile(inner))], store_partial(c))
+        for c in range(chunks):
+            sum_copy(c).wait_recv()
+            held[c][0] = (
+                partial[:, rows_of(c)] + remote_sum[:, rows_of(c)].astype(jnp.float32)
+            ).astype(jnp.bfloat16)
+            spread(held_spread, c, 0, sent)
+            follow(c, picked)
+        end(picked)
+
+    sent = []
+
+    @pl.when(jnp.logical_not(is_outer))
+    def _():
+        for c in range(chunks):
+            start(raw(c, inner, 0, near))
+        for c in range(early):
+            start(raw(c, inner, 1, facing))
+        picked = set_weights()
+        for q in range(PIECES):
+            tile_copy(q).wait_recv()
+            spread(tile_spread, q, 0, sent)
+            if q >= 1:
+                for label in range(1, n_chips):
+                    tile_arrive(q - 1, label)
+                    spread(tile_spread, q - 1, label, sent)
+        local[3].wait()
+        local[4].wait()
+
+        def pass_on(c):
+            raw(c, outer, 0, near).wait_recv()
+            start(raw(c, outer, 2, facing))
+            if c + early < chunks:
+                start(raw(c + early, inner, 1, facing))
+
+        pass_on(0)
+        for label in range(1, n_chips):
+            tile_arrive(PIECES - 1, label)
+            spread(tile_spread, PIECES - 1, label, sent)
+        pass_on(1)
+        for q in range(PIECES):
+            for label in range(n_chips):
+                tile_arrive(q, n_chips + label)
+        for c in range(chunks):
+            if c + 2 < chunks:
+                pass_on(c + 2)
+            raw(c, across, 1, facing).wait_recv()
+            raw(c, beyond, 2, facing).wait_recv()
+            product(c, [(across, far_tile(0)), (beyond, far_tile(1))], store_sum(c))
+            start(sum_copy(c))
+            product(c, [(plane, own_tile(plane)) for plane in (inner, outer, across, beyond)], store_held(c))
+            spread(held_spread, c, 0, sent)
+            follow(c, picked)
+        end(picked)
+
+
+def line_call(mesh, coefficients, couplings, exc_list, counts, beta_tiles):
+    n_alpha, n_beta = mesh.shape["alpha"], mesh.shape["beta"]
+    order = couplings.shape[1]
+    rows, columns = coefficients.shape
+    n_blocks = rows // order
+    heights = [order * share // sum(SHARES) for share in SHARES]
+    chunks = len(heights)
+    hbm = pl.BlockSpec(memory_space=pl.ANY)
+    dma = pltpu.SemaphoreType.DMA
+    return pl.pallas_call(
+        functools.partial(line_kernel, n_alpha, n_beta, (n_alpha // 2).bit_length() - 1, heights, 3),
+        out_shape=pltpu.VMEM((rows, columns), jnp.float32),
+        in_specs=[hbm] * 5,
+        out_specs=pl.BlockSpec(memory_space=pltpu.VMEM),
+        scratch_shapes=[
+            pltpu.SMEM((3, n_alpha, n_alpha), jnp.int32),
+            pltpu.SMEM((n_alpha, n_alpha), jnp.int32),
+            pltpu.VMEM(couplings.shape, jnp.bfloat16),
+            pltpu.VMEM((order // LANES, rows, n_alpha * LANES), jnp.bfloat16),
+            pltpu.VMEM(beta_tiles.shape, jnp.bfloat16),
+            pltpu.VMEM((n_beta, n_blocks, order, columns), jnp.bfloat16),
+            pltpu.VMEM((2 * columns, columns), jnp.bfloat16),
+            pltpu.VMEM((n_blocks, order, columns), jnp.float32),
+            pltpu.VMEM((n_blocks, order, columns), jnp.bfloat16),
+            [pltpu.VMEM((n_alpha, n_blocks, height, columns), jnp.bfloat16) for height in heights],
+            pltpu.VMEM((order // LANES, n_alpha * LANES, columns), jnp.bfloat16),
+            dma((5,)),
+            dma((3, chunks)),
+            dma((n_beta, chunks)),
+            dma((chunks,)),
+            dma((chunks,)),
+            dma((PIECES,)),
+            dma((PIECES,)),
+            dma((PIECES, n_alpha)),
+            dma((PIECES, n_alpha)),
+            dma((chunks, n_alpha)),
+            dma((chunks, n_alpha)),
+        ],
+        compiler_params=pltpu.CompilerParams(
+            collective_id=0, has_side_effects=True, vmem_limit_bytes=60 * 2**20
+        ),
+    )(
+        exc_list.transpose(2, 0, 1),
+        counts,
+        couplings,
+        coefficients.reshape(n_blocks, order, columns),
+        beta_tiles,
+    )
+
+
 def solution(mesh):
     n_alpha, n_beta = mesh.shape["alpha"], mesh.shape["beta"]
     n_chips = n_alpha // 2
@@ -199,6 +516,8 @@
         rows, columns = coefficients.shape
         n_blocks = rows // order
         n_stops = beta_tiles.shape[0]
+        if n_beta == n_stops == 4:
+            return line_call(mesh, coefficients, couplings, exc_list, counts, beta_tiles)
         widths, _ = split(columns)
         chunks = len(widths)
         vmem, smem = pl.BlockSpec(memory_space=pltpu.VMEM), pl.BlockSpec(memory_space=pltpu.SMEM)

time: 98.6 us -> 107 us (1.085); the launches traced: 98.3 us -> 106 us
  Pallas kernels: 93.1 us -> 104 us
  local copies, waits for them, and re-layouts: 5.16 us -> 1.32 us
    pallas_call x1, Pallas kernels: 93.1 us -> 104 us  [line_call(): pl.pallas_call(functools.partial(line_kernel, n_alpha, n_beta, (n_alpha /...]
    unnamed x9 -> x1, local copies, waits for them, and re-layouts: 5.16 us -> 1.32 us
where the time goes in v1:
time: 107 us; the launch traced here: 106 us
  Pallas kernels  104 us (97%)
  local copies, waits for them, and re-layouts  1.32 us (1%)
    pallas_call x1, Pallas kernels, line_call(): pl.pallas_call(functools.partial(line_kernel, n_alpha, n_beta, (n_alpha /...  104 us

profile of v1, /device:TPU:0, one launch (start us, length us, event | category | flops | bytes accessed | tf_op | source)
XLA Modules:
  0.0 105.6 jit_solution(5516246851539088628)
XLA Ops:
  0.0 104.3 %shard_map.55 = f32[512,1024]{1,0:T(8,128)S(1)} custom-call(s32[3,8,8]{2,1,0:T(8,128)} %bitcast.3, s32[8,8]{1,0:T(8,128)} %counts_hbm.1, bf16[8,256,256]{2,1,0:T(8,128)(2,1)} %coupling_hbm.1, bf16[2,256,1024]{2,1,0:T(8,128)(2,1)} %bitcast.2, bf16[4,1024,1024]{2,1,0:T(8,128)(2,1)} %b_hbm.1), custom_call_target="tpu_custom_call" | custom-call | tf_op jit(solution)/shard_map/pallas_call | solution.py:468
  104.3 1.3 %copy.7 = f32[512,1024]{1,0:T(8,128)} copy(f32[512,1024]{1,0:T(8,128)S(1)} %shard_map.55) | data formatting | bytes 4194304

commit v2 on v1

--- a/solution.py
+++ b/solution.py
@@ -11,7 +11,7 @@
 WIDTHS = (1, 2, 2, 2, 1)
 TILE = 256
 AHEAD = 1
-SHARES = (4, 4, 4, 2, 2)
+SHARES = (1, 1, 1, 1, 1, 1, 1, 1)
 PIECES = 4
 LANES = 128
 
@@ -369,17 +369,16 @@
                     out_ref[:, at] += value
 
     def follow(c, picked):
-        if c >= 1:
-            for label in range(1, n_chips):
-                relay(c - 1, label)
-        if c >= 2:
-            finish(c - 2, picked)
+        for label in range(1, n_chips):
+            behind = c - label.bit_count()
+            if 0 <= behind < chunks:
+                relay(behind, label)
+        if 0 <= c - rounds - 1 < chunks:
+            finish(c - rounds - 1, picked)
 
     def end(picked):
-        for label in range(1, n_chips):
-            relay(chunks - 1, label)
-        for c in range(max(chunks - 2, 0), chunks):
-            finish(c, picked)
+        for c in range(chunks, chunks + rounds + 1):
+            follow(c, picked)
         for copy in sent:
             copy.wait_send()
 
@@ -419,33 +418,36 @@
         for c in range(early):
             start(raw(c, inner, 1, facing))
         picked = set_weights()
+        def tile_follow(q):
+            for label in range(1, n_chips):
+                behind = q - label.bit_count()
+                if 0 <= behind < PIECES:
+                    tile_arrive(behind, label)
+                    spread(tile_spread, behind, label, sent)
+
+        def pass_on(c):
+            if c < chunks:
+                raw(c, outer, 0, near).wait_recv()
+                start(raw(c, outer, 2, facing))
+                if c >= 1 and c - 1 + early < chunks:
+                    start(raw(c - 1 + early, inner, 1, facing))
+
         for q in range(PIECES):
             tile_copy(q).wait_recv()
             spread(tile_spread, q, 0, sent)
-            if q >= 1:
-                for label in range(1, n_chips):
-                    tile_arrive(q - 1, label)
-                    spread(tile_spread, q - 1, label, sent)
+            tile_follow(q)
+        pass_on(0)
+        tile_follow(PIECES)
+        pass_on(1)
+        for q in range(PIECES + 1, PIECES + rounds):
+            tile_follow(q)
+        pass_on(2)
         local[3].wait()
         local[4].wait()
-
-        def pass_on(c):
-            raw(c, outer, 0, near).wait_recv()
-            start(raw(c, outer, 2, facing))
-            if c + early < chunks:
-                start(raw(c + early, inner, 1, facing))
-
-        pass_on(0)
-        for label in range(1, n_chips):
-            tile_arrive(PIECES - 1, label)
-            spread(tile_spread, PIECES - 1, label, sent)
-        pass_on(1)
         for q in range(PIECES):
             for label in range(n_chips):
                 tile_arrive(q, n_chips + label)
         for c in range(chunks):
-            if c + 2 < chunks:
-                pass_on(c + 2)
             raw(c, across, 1, facing).wait_recv()
             raw(c, beyond, 2, facing).wait_recv()
             product(c, [(across, far_tile(0)), (beyond, far_tile(1))], store_sum(c))
@@ -453,6 +455,7 @@
             product(c, [(plane, own_tile(plane)) for plane in (inner, outer, across, beyond)], store_held(c))
             spread(held_spread, c, 0, sent)
             follow(c, picked)
+            pass_on(c + 3)
         end(picked)
 
 
@@ -466,7 +469,7 @@
     hbm = pl.BlockSpec(memory_space=pl.ANY)
     dma = pltpu.SemaphoreType.DMA
     return pl.pallas_call(
-        functools.partial(line_kernel, n_alpha, n_beta, (n_alpha // 2).bit_length() - 1, heights, 3),
+        functools.partial(line_kernel, n_alpha, n_beta, (n_alpha // 2).bit_length() - 1, heights, 6),
         out_shape=pltpu.VMEM((rows, columns), jnp.float32),
         in_specs=[hbm] * 5,
         out_specs=pl.BlockSpec(memory_space=pltpu.VMEM),

time: 107 us -> 85.1 us (0.80)
  Pallas kernels: 104 us -> 82.9 us
    pallas_call x1, Pallas kernels: 104 us -> 82.9 us  [line_call(): pl.pallas_call(functools.partial(line_kernel, n_alpha, n_beta, (n_alpha /...]
where the time goes in v2:
time: 85.1 us; the launch traced here: 84.2 us
  Pallas kernels  82.9 us (97%)
  local copies, waits for them, and re-layouts  1.32 us (2%)
    pallas_call x1, Pallas kernels, line_call(): pl.pallas_call(functools.partial(line_kernel, n_alpha, n_beta, (n_alpha /...  82.9 us

profile of v2, /device:TPU:0, one launch (start us, length us, event | category | flops | bytes accessed | tf_op | source)
XLA Modules:
  0.0 84.2 jit_solution(1535594973600388692)
XLA Ops:
  0.0 82.9 %shard_map.55 = f32[512,1024]{1,0:T(8,128)S(1)} custom-call(s32[3,8,8]{2,1,0:T(8,128)} %bitcast.3, s32[8,8]{1,0:T(8,128)} %counts_hbm.1, bf16[8,256,256]{2,1,0:T(8,128)(2,1)} %coupling_hbm.1, bf16[2,256,1024]{2,1,0:T(8,128)(2,1)} %bitcast.2, bf16[4,1024,1024]{2,1,0:T(8,128)(2,1)} %b_hbm.1), custom_call_target="tpu_custom_call" | custom-call | tf_op jit(solution)/shard_map/pallas_call | solution.py:471
  82.9 1.3 %copy.7 = f32[512,1024]{1,0:T(8,128)} copy(f32[512,1024]{1,0:T(8,128)S(1)} %shard_map.55) | data formatting | bytes 4194304

commit v3 on v2

--- a/solution.py
+++ b/solution.py
@@ -13,6 +13,10 @@
 AHEAD = 1
 SHARES = (1, 1, 1, 1, 1, 1, 1, 1)
 PIECES = 4
+LAG = 2
+RAW = 2
+FIRST = 4
+SECOND = 6
 LANES = 128
 
 
@@ -193,10 +197,11 @@
 
 
 def line_kernel(
-    n_alpha, n_beta, rounds, heights, early,
+    n_alpha, n_beta, rounds, heights,
     exc_hbm, counts_hbm, coupling_hbm, c_hbm, b_hbm, out_ref,
     exc_ref, counts_ref, coupling_ref, weights, tiles, blocks, outer_tiles, partial, remote_sum, held, gathered,
-    in_sem, raw_send, raw_recv, sum_send, sum_recv, tile_send, tile_recv, spread_send, spread_recv, send_sem, recv_sem,
+    in_sem, raw_send, raw_recv, sum_send, sum_recv, tile_send, tile_recv, spread_send, spread_recv, spread_last,
+    send_sem, recv_sem,
 ):
     n_chips = n_alpha // 2
     n_blocks, order, columns = c_hbm.shape
@@ -258,45 +263,56 @@
 
     def raw(c, plane, kind, device):
         source = c_hbm.at[:, rows_of(c)] if kind < 2 else blocks.at[plane, :, rows_of(c)]
-        return remote(
-            source, blocks.at[plane, :, rows_of(c)], raw_send.at[kind, c], raw_recv.at[plane, c], device
-        )
+        return remote(source, blocks.at[plane, :, rows_of(c)], raw_send.at[kind], raw_recv.at[plane, c], device)
 
     def sum_copy(c):
         here = remote_sum.at[:, rows_of(c)]
-        return remote(here, here, sum_send.at[c], sum_recv.at[c], near)
+        return remote(here, here, sum_send, sum_recv.at[c], near)
 
     piece = 2 * b_hbm.shape[1] // n_alpha
     part = piece // PIECES
+
+    def part_of(label, q):
+        return pl.ds(pl.multiple_of(sources[label] * piece + q * part, part), part)
 
     def tile_copy(q):
         row = alpha * piece + q * part
         which = lax.div(row, b_hbm.shape[1])
         tile = (1 - which) * 2 + which * (1 + 2 * side)
         source = b_hbm.at[tile, pl.ds(pl.multiple_of(lax.rem(row, b_hbm.shape[1]), part), part)]
-        target = outer_tiles.at[pl.ds(pl.multiple_of(row, part), part)]
-        return remote(source, target, tile_send.at[q], tile_recv.at[q], near)
+        return remote(source, outer_tiles.at[part_of(0, q)], tile_send, tile_recv.at[q], near)
+
+    def group_of(label):
+        return label.bit_count() - 1 if label < n_chips else rounds
 
     def tile_spread(q, label, target, device):
-        here = outer_tiles.at[pl.ds(pl.multiple_of(sources[label] * piece + q * part, part), part)]
-        return remote(here, here, spread_send.at[q, target], spread_recv.at[q, target], device)
+        here = outer_tiles.at[part_of(label, q)]
+        recv = spread_recv.at[q, group_of(target)] if target < n_chips else spread_last
+        return remote(here, here, spread_send, recv, device)
 
     def held_spread(c, label, target, device):
-        return remote(held[c].at[label], held[c].at[target], send_sem.at[c, target], recv_sem.at[c, target], device)
-
-    def spread(make, index, label, sent):
+        return remote(
+            held[c].at[label], held[c].at[target], send_sem.at[c], recv_sem.at[c, group_of(target)], device
+        )
+
+    def spread(make, index, label):
         for step in range(label.bit_length(), rounds):
-            sent.append(make(index, label, label + 2**step, neighbours[step]))
-            sent[-1].start()
-        sent.append(make(index, label, n_chips + label, sibling))
-        sent[-1].start()
-
-    def arrive(make, index, label):
-        make(index, label, label, sibling).wait_recv()
-
-    def tile_arrive(q, label):
-        here = outer_tiles.at[pl.ds(pl.multiple_of(sources[label] * piece + q * part, part), part)]
-        remote(here, here, spread_send.at[q, label], spread_recv.at[q, label], sibling).wait_recv()
+            make(index, label, label + 2**step, neighbours[step]).start()
+        make(index, label, n_chips + label, sibling).start()
+
+    labels_of = [range(1, n_chips - 1), range(n_chips - 1, n_chips), range(n_chips, n_alpha)]
+
+    def tile_relay(q, group):
+        count = len(labels_of[group]) * part
+        here = outer_tiles.at[pl.ds(0, count)]
+        remote(here, here, spread_send, spread_recv.at[q, group], sibling).wait_recv()
+        for label in labels_of[group]:
+            spread(tile_spread, q, label)
+
+    def held_arrive(c, group):
+        labels = labels_of[group]
+        here = held[c].at[pl.ds(labels[0], len(labels))]
+        remote(here, here, send_sem.at[c], recv_sem.at[c, group], sibling).wait_recv()
 
     def set_weights():
         for copy in local[:3]:
@@ -316,45 +332,46 @@
                     ]
         return picked
 
-    def product(c, terms, store):
+    def product(first, count, planes, tile, store, before=False):
+        at_rows = pl.ds(offsets[first], sum(heights[first : first + count]))
+
         @pl.loop(0, columns // TILE)
         def _(n):
             at = pl.ds(pl.multiple_of(n * TILE, TILE), TILE)
             value = None
-            for plane, right in terms:
-                left = blocks[plane, :, rows_of(c)].reshape(n_blocks * heights[c], columns)
-                term = jnp.dot(left, right(at), preferred_element_type=jnp.float32)
+            for k, plane in enumerate(planes):
+                left = blocks[plane, :, at_rows].reshape(n_blocks * at_rows.size, columns)
+                term = jnp.dot(left, tile(k, plane, at), preferred_element_type=jnp.float32)
                 value = term if value is None else value + term
-            store(at, value)
-
-    def own_tile(plane):
-        return lambda at: tiles[distance(plane), :, at]
-
-    def far_tile(k):
-        return lambda at: outer_tiles[pl.ds(k * columns, columns), at]
+            value = value.reshape(n_blocks, at_rows.size, TILE)
+            if before:
+                value = value + partial[:, at_rows, at]
+            store(at_rows, at, value)
+
+    def own_tile(k, plane, at):
+        return tiles[distance(plane), :, at]
+
+    def far_tile(k, plane, at):
+        return outer_tiles[pl.ds(k * columns, columns), at]
 
     def store_held(c):
-        def store(at, value):
-            held[c][0, :, :, at] = value.astype(jnp.bfloat16).reshape(n_blocks, heights[c], TILE)
+        def store(at_rows, at, value):
+            held[c][0, :, :, at] = value.astype(jnp.bfloat16)
         return store
 
-    def store_sum(c):
-        def store(at, value):
-            remote_sum[:, rows_of(c), at] = value.astype(jnp.bfloat16).reshape(n_blocks, heights[c], TILE)
-        return store
-
-    def store_partial(c):
-        def store(at, value):
-            partial[:, rows_of(c), at] = value.reshape(n_blocks, heights[c], TILE)
-        return store
-
-    def relay(c, label):
-        arrive(held_spread, c, label)
-        spread(held_spread, c, label, sent)
+    def store_sum(at_rows, at, value):
+        remote_sum[:, at_rows, at] = value.astype(jnp.bfloat16)
+
+    def store_partial(at_rows, at, value):
+        partial[:, at_rows, at] = value
+
+    def relay(c, group):
+        held_arrive(c, group)
+        for label in labels_of[group]:
+            spread(held_spread, c, label)
 
     def finish(c, picked):
-        for label in range(n_chips):
-            arrive(held_spread, c, n_chips + label)
+        held_arrive(c, rounds)
         half, within = offsets[c] // LANES, offsets[c] % LANES
         for slot in range(n_alpha):
             gathered[half, pl.ds(slot * LANES + within, heights[c])] = held[c][slot, picked[slot]]
@@ -369,94 +386,158 @@
                     out_ref[:, at] += value
 
     def follow(c, picked):
-        for label in range(1, n_chips):
-            behind = c - label.bit_count()
+        for group in range(rounds):
+            behind = c - LAG * (group + 1)
             if 0 <= behind < chunks:
-                relay(behind, label)
-        if 0 <= c - rounds - 1 < chunks:
-            finish(c - rounds - 1, picked)
+                relay(behind, group)
+        if 0 <= c - LAG * rounds - 1 < chunks:
+            finish(c - LAG * rounds - 1, picked)
 
     def end(picked):
-        for c in range(chunks, chunks + rounds + 1):
+        for c in range(chunks, chunks + LAG * rounds + 1):
             follow(c, picked)
-        for copy in sent:
-            copy.wait_send()
-
-    sent = []
-
-    def start(copy):
-        sent.append(copy)
-        copy.start()
+        for c in range(chunks):
+            here = held[c].at[pl.ds(1, n_alpha - 1)]
+            remote(here, here, send_sem.at[c], recv_sem.at[c, 0], sibling).wait_send()
+
+    def sent(ref, sem):
+        remote(ref, ref, sem, sum_recv.at[0], near).wait_send()
 
     @pl.when(is_outer)
     def _():
-        for q in range(PIECES):
-            start(tile_copy(q))
-        for c in range(chunks):
-            start(raw(c, outer, 0, near))
+        def own(c):
+            raw(c, outer, 0, near).start()
+
+        tile_copy(0).start()
+        tile_copy(1).start()
+        own(0)
+        for q in range(2, PIECES):
+            tile_copy(q).start()
+        for c in range(1, chunks):
+            own(c)
         picked = set_weights()
         local[3].wait()
         local[4].wait()
-        for c in range(chunks):
-            raw(c, inner, 0, near).wait_recv()
-            product(c, [(outer, own_tile(outer)), (inner, own_tile(inner))], store_partial(c))
-        for c in range(chunks):
+
+        def prepare(c):
+            for k in range(c, c + 2):
+                raw(k, inner, 0, near).wait_recv()
+            product(c, 2, (outer, inner), own_tile, store_partial)
+
+        def finish_raw(c):
+            raw(c, across, 0, near).wait_recv()
+            raw(c, beyond, 0, near).wait_recv()
+            product(c, 1, (across, beyond), own_tile, store_held(c), before=True)
+            spread(held_spread, c, 0)
+
+        prepare(0)
+        prepare(2)
+        finish_raw(0)
+        prepare(4)
+        finish_raw(1)
+        for c in range(RAW, chunks):
             sum_copy(c).wait_recv()
+            if c == 6:
+                prepare(6)
             held[c][0] = (
                 partial[:, rows_of(c)] + remote_sum[:, rows_of(c)].astype(jnp.float32)
             ).astype(jnp.bfloat16)
-            spread(held_spread, c, 0, sent)
+            spread(held_spread, c, 0)
             follow(c, picked)
         end(picked)
-
-    sent = []
+        sent(outer_tiles.at[pl.ds(0, piece)], tile_send)
+        sent(blocks.at[outer], raw_send.at[0])
 
     @pl.when(jnp.logical_not(is_outer))
     def _():
-        for c in range(chunks):
-            start(raw(c, inner, 0, near))
-        for c in range(early):
-            start(raw(c, inner, 1, facing))
+        def own_near(c):
+            raw(c, inner, 0, near).start()
+
+        def own_facing(c):
+            raw(c, inner, 1, facing).start()
+
+        for c in range(FIRST):
+            own_near(c)
+            own_facing(c)
+        own_near(FIRST)
         picked = set_weights()
-        def tile_follow(q):
-            for label in range(1, n_chips):
-                behind = q - label.bit_count()
-                if 0 <= behind < PIECES:
-                    tile_arrive(behind, label)
-                    spread(tile_spread, behind, label, sent)
+        local[3].wait()
+        local[4].wait()
+
+        def prepare(c):
+            for k in range(c, c + 2):
+                raw(k, across, 1, facing).wait_recv()
+            product(c, 2, (inner, across), own_tile, store_partial)
 
         def pass_on(c):
             if c < chunks:
                 raw(c, outer, 0, near).wait_recv()
-                start(raw(c, outer, 2, facing))
-                if c >= 1 and c - 1 + early < chunks:
-                    start(raw(c - 1 + early, inner, 1, facing))
-
-        for q in range(PIECES):
+                if c >= SECOND:
+                    own_facing(c)
+                raw(c, outer, 2, facing).start()
+
+        def tile_own(q):
             tile_copy(q).wait_recv()
-            spread(tile_spread, q, 0, sent)
-            tile_follow(q)
+            spread(tile_spread, q, 0)
+
+        def finish_held(c):
+            product(c, 1, (outer, beyond), own_tile, store_held(c), before=True)
+            spread(held_spread, c, 0)
+
+        def send_beyond(c):
+            raw(c, beyond, 2, facing).wait_recv()
+            raw(c, beyond, 3, near).start()
+
+        tile_own(0)
+        tile_own(1)
+        prepare(0)
+        for c in range(RAW):
+            raw(c, across, 3, near).start()
         pass_on(0)
-        tile_follow(PIECES)
+        for c in range(FIRST, SECOND):
+            own_facing(c)
+        tile_relay(0, 0)
+        tile_own(2)
+        tile_relay(1, 0)
+        prepare(2)
+        tile_own(3)
+        tile_relay(0, 1)
+        send_beyond(0)
+        for c in range(FIRST + 1, SECOND + 1):
+            own_near(c)
+        tile_relay(2, 0)
         pass_on(1)
-        for q in range(PIECES + 1, PIECES + rounds):
-            tile_follow(q)
+        tile_relay(1, 1)
+        tile_relay(3, 0)
         pass_on(2)
-        local[3].wait()
-        local[4].wait()
-        for q in range(PIECES):
-            for label in range(n_chips):
-                tile_arrive(q, n_chips + label)
-        for c in range(chunks):
-            raw(c, across, 1, facing).wait_recv()
+        finish_held(0)
+        tile_relay(2, 1)
+        prepare(4)
+        pass_on(3)
+        tile_relay(3, 1)
+        send_beyond(1)
+        finish_held(1)
+        here = outer_tiles.at[pl.ds(0, n_chips * piece)]
+        remote(here, here, spread_send, spread_last, sibling).wait_recv()
+        for c in range(RAW, chunks):
+            if c >= SECOND:
+                raw(c, across, 1, facing).wait_recv()
             raw(c, beyond, 2, facing).wait_recv()
-            product(c, [(across, far_tile(0)), (beyond, far_tile(1))], store_sum(c))
-            start(sum_copy(c))
-            product(c, [(plane, own_tile(plane)) for plane in (inner, outer, across, beyond)], store_held(c))
-            spread(held_spread, c, 0, sent)
+            product(c, 1, (across, beyond), far_tile, store_sum)
+            sum_copy(c).start()
+            if c == RAW + 1:
+                own_near(chunks - 1)
+            pass_on(c + 2)
+            if c >= SECOND:
+                product(c, 1, (inner, across), own_tile, store_partial)
+            finish_held(c)
             follow(c, picked)
-            pass_on(c + 3)
         end(picked)
+        sent(outer_tiles.at[pl.ds(0, (n_alpha - 1) * piece)], spread_send)
+        sent(remote_sum.at[:, pl.ds(offsets[RAW], order - offsets[RAW])], sum_send)
+        for kind in range(3):
+            sent(blocks.at[inner], raw_send.at[kind])
+        sent(blocks.at[inner, :, pl.ds(0, offsets[2 * RAW])], raw_send.at[3])
 
 
 def line_call(mesh, coefficients, couplings, exc_list, counts, beta_tiles):
@@ -466,10 +547,11 @@
     n_blocks = rows // order
     heights = [order * share // sum(SHARES) for share in SHARES]
     chunks = len(heights)
+    rounds = (n_alpha // 2).bit_length() - 1
     hbm = pl.BlockSpec(memory_space=pl.ANY)
     dma = pltpu.SemaphoreType.DMA
     return pl.pallas_call(
-        functools.partial(line_kernel, n_alpha, n_beta, (n_alpha // 2).bit_length() - 1, heights, 6),
+        functools.partial(line_kernel, n_alpha, n_beta, rounds, heights),
         out_shape=pltpu.VMEM((rows, columns), jnp.float32),
         in_specs=[hbm] * 5,
         out_specs=pl.BlockSpec(memory_space=pltpu.VMEM),
@@ -486,16 +568,17 @@
             [pltpu.VMEM((n_alpha, n_blocks, height, columns), jnp.bfloat16) for height in heights],
             pltpu.VMEM((order // LANES, n_alpha * LANES, columns), jnp.bfloat16),
             dma((5,)),
-            dma((3, chunks)),
+            dma((4,)),
             dma((n_beta, chunks)),
+            dma(()),
             dma((chunks,)),
+            dma(()),
+            dma((PIECES,)),
+            dma(()),
+            dma((PIECES, rounds)),
+            dma(()),
             dma((chunks,)),
-            dma((PIECES,)),
-            dma((PIECES,)),
-            dma((PIECES, n_alpha)),
-            dma((PIECES, n_alpha)),
-            dma((chunks, n_alpha)),
-            dma((chunks, n_alpha)),
+            dma((chunks, rounds + 1)),
         ],
         compiler_params=pltpu.CompilerParams(
             collective_id=0, has_side_effects=True, vmem_limit_bytes=60 * 2**20
@@ -519,7 +602,7 @@
         rows, columns = coefficients.shape
         n_blocks = rows // order
         n_stops = beta_tiles.shape[0]
-        if n_beta == n_stops == 4:
+        if n_alpha == 8 and n_beta == n_stops == 4:
             return line_call(mesh, coefficients, couplings, exc_list, counts, beta_tiles)
         widths, _ = split(columns)
         chunks = len(widths)

time: 85.1 us -> 74.9 us (0.88)
  Pallas kernels: 82.9 us -> 73.5 us
    pallas_call x1, Pallas kernels: 82.9 us -> 73.5 us  [line_call(): pl.pallas_call(functools.partial(line_kernel, n_alpha, n_beta, rounds, he...]
where the time goes in v3:
time: 74.9 us; the launch traced here: 74.8 us
  Pallas kernels  73.5 us (98%)
  local copies, waits for them, and re-layouts  1.32 us (2%)
    pallas_call x1, Pallas kernels, line_call(): pl.pallas_call(functools.partial(line_kernel, n_alpha, n_beta, rounds, he...  73.5 us

profile of v3, /device:TPU:0, one launch (start us, length us, event | category | flops | bytes accessed | tf_op | source)
XLA Modules:
  0.0 74.8 jit_solution(9601999542318919009)
XLA Ops:
  0.0 73.5 %shard_map.55 = f32[512,1024]{1,0:T(8,128)S(1)} custom-call(s32[3,8,8]{2,1,0:T(8,128)} %bitcast.3, s32[8,8]{1,0:T(8,128)} %counts_hbm.1, bf16[8,256,256]{2,1,0:T(8,128)(2,1)} %coupling_hbm.1, bf16[2,256,1024]{2,1,0:T(8,128)(2,1)} %bitcast.2, bf16[4,1024,1024]{2,1,0:T(8,128)(2,1)} %b_hbm.1), custom_call_target="tpu_custom_call" | custom-call | tf_op jit(solution)/shard_map/pallas_call | solution.py:553
  73.5 1.3 %copy.7 = f32[512,1024]{1,0:T(8,128)} copy(f32[512,1024]{1,0:T(8,128)S(1)} %shard_map.55) | data formatting | bytes 4194304

commit v4 on v3

--- a/solution.py
+++ b/solution.py
@@ -17,7 +17,7 @@
 RAW = 2
 FIRST = 4
 SECOND = 6
-LANES = 128
+LANES = 64
 
 
 def split(columns):
@@ -385,33 +385,44 @@
                 else:
                     out_ref[:, at] += value
 
-    def follow(c, picked):
+    def advance(group, last, picked):
+        while progress[group] <= min(last, chunks - 1):
+            if group < rounds:
+                relay(progress[group], group)
+            else:
+                finish(progress[group], picked)
+            progress[group] += 1
+
+    def follow(c, lag, picked):
         for group in range(rounds):
-            behind = c - LAG * (group + 1)
-            if 0 <= behind < chunks:
-                relay(behind, group)
-        if 0 <= c - LAG * rounds - 1 < chunks:
-            finish(c - LAG * rounds - 1, picked)
+            advance(group, c - lag - LAG * group, picked)
+        advance(rounds, c - lag - LAG * (rounds - 1) - 1, picked)
 
     def end(picked):
-        for c in range(chunks, chunks + LAG * rounds + 1):
-            follow(c, picked)
+        advance(rounds, chunks - 1 - 2 * LAG, picked)
+        for group in range(rounds - 1):
+            advance(group, chunks - 1, picked)
+        advance(rounds - 1, chunks - 1 - LAG, picked)
+        advance(rounds, chunks - 1 - LAG, picked)
+        advance(rounds - 1, chunks - 1, picked)
+        advance(rounds, chunks - 1, picked)
         for c in range(chunks):
             here = held[c].at[pl.ds(1, n_alpha - 1)]
             remote(here, here, send_sem.at[c], recv_sem.at[c, 0], sibling).wait_send()
 
     def sent(ref, sem):
         remote(ref, ref, sem, sum_recv.at[0], near).wait_send()
+
+    progress = [0] * (rounds + 1)
 
     @pl.when(is_outer)
     def _():
         def own(c):
             raw(c, outer, 0, near).start()
 
-        tile_copy(0).start()
-        tile_copy(1).start()
-        own(0)
-        for q in range(2, PIECES):
+        for q in range(PIECES):
+            if q == PIECES // 2:
+                own(0)
             tile_copy(q).start()
         for c in range(1, chunks):
             own(c)
@@ -419,10 +430,10 @@
         local[3].wait()
         local[4].wait()
 
-        def prepare(c):
-            for k in range(c, c + 2):
+        def prepare(c, count):
+            for k in range(c, c + count):
                 raw(k, inner, 0, near).wait_recv()
-            product(c, 2, (outer, inner), own_tile, store_partial)
+            product(c, count, (outer, inner), own_tile, store_partial)
 
         def finish_raw(c):
             raw(c, across, 0, near).wait_recv()
@@ -430,23 +441,27 @@
             product(c, 1, (across, beyond), own_tile, store_held(c), before=True)
             spread(held_spread, c, 0)
 
-        prepare(0)
-        prepare(2)
+        prepare(0, 2)
+        prepare(2, 2)
         finish_raw(0)
-        prepare(4)
         finish_raw(1)
+        follow(1, 1, picked)
         for c in range(RAW, chunks):
+            if c == 4:
+                prepare(c, 2)
+            if c >= SECOND:
+                prepare(c, 1)
             sum_copy(c).wait_recv()
-            if c == 6:
-                prepare(6)
             held[c][0] = (
                 partial[:, rows_of(c)] + remote_sum[:, rows_of(c)].astype(jnp.float32)
             ).astype(jnp.bfloat16)
             spread(held_spread, c, 0)
-            follow(c, picked)
+            follow(c, 1 if c <= RAW + 1 else LAG, picked)
         end(picked)
         sent(outer_tiles.at[pl.ds(0, piece)], tile_send)
         sent(blocks.at[outer], raw_send.at[0])
+
+    progress = [0] * (rounds + 1)
 
     @pl.when(jnp.logical_not(is_outer))
     def _():
@@ -457,9 +472,9 @@
             raw(c, inner, 1, facing).start()
 
         for c in range(FIRST):
-            own_near(c)
+            if c < 3:
+                own_near(c)
             own_facing(c)
-        own_near(FIRST)
         picked = set_weights()
         local[3].wait()
         local[4].wait()
@@ -472,9 +487,9 @@
         def pass_on(c):
             if c < chunks:
                 raw(c, outer, 0, near).wait_recv()
-                if c >= SECOND:
-                    own_facing(c)
                 raw(c, outer, 2, facing).start()
+                if SECOND <= c + 1 < chunks:
+                    own_facing(c + 1)
 
         def tile_own(q):
             tile_copy(q).wait_recv()
@@ -488,14 +503,25 @@
             raw(c, beyond, 2, facing).wait_recv()
             raw(c, beyond, 3, near).start()
 
+        def hold(c, lag):
+            if c >= FIRST and c % 2 == 0:
+                product(c, 2, (inner, across), own_tile, store_partial)
+            finish_held(c)
+            follow(c, lag, picked)
+
+        def send_across(c):
+            raw(c, across, 1, facing).wait_recv()
+            raw(c, across, 3, near).start()
+
         tile_own(0)
         tile_own(1)
-        prepare(0)
-        for c in range(RAW):
-            raw(c, across, 3, near).start()
+        send_across(0)
+        send_across(1)
+        own_near(3)
+        product(0, 2, (inner, across), own_tile, store_partial)
         pass_on(0)
-        for c in range(FIRST, SECOND):
-            own_facing(c)
+        own_facing(4)
+        own_facing(5)
         tile_relay(0, 0)
         tile_own(2)
         tile_relay(1, 0)
@@ -503,35 +529,37 @@
         tile_own(3)
         tile_relay(0, 1)
         send_beyond(0)
-        for c in range(FIRST + 1, SECOND + 1):
-            own_near(c)
+        own_near(4)
+        own_near(5)
         tile_relay(2, 0)
         pass_on(1)
         tile_relay(1, 1)
+        product(0, 1, (outer, beyond), own_tile, store_held(0), before=True)
         tile_relay(3, 0)
         pass_on(2)
-        finish_held(0)
+        spread(held_spread, 0, 0)
         tile_relay(2, 1)
-        prepare(4)
         pass_on(3)
+        send_beyond(1)
         tile_relay(3, 1)
-        send_beyond(1)
-        finish_held(1)
+        hold(1, 1)
+        pass_on(4)
         here = outer_tiles.at[pl.ds(0, n_chips * piece)]
         remote(here, here, spread_send, spread_last, sibling).wait_recv()
         for c in range(RAW, chunks):
-            if c >= SECOND:
+            if c >= FIRST:
                 raw(c, across, 1, facing).wait_recv()
             raw(c, beyond, 2, facing).wait_recv()
             product(c, 1, (across, beyond), far_tile, store_sum)
             sum_copy(c).start()
-            if c == RAW + 1:
-                own_near(chunks - 1)
-            pass_on(c + 2)
-            if c >= SECOND:
-                product(c, 1, (inner, across), own_tile, store_partial)
-            finish_held(c)
-            follow(c, picked)
+            if SECOND <= c + 1 < chunks:
+                own_near(c + 1)
+            pass_on(c + 3)
+            if c == RAW:
+                hold(c, 1)
+            elif c > RAW + 1:
+                hold(c - 1, LAG)
+        hold(chunks - 1, LAG)
         end(picked)
         sent(outer_tiles.at[pl.ds(0, (n_alpha - 1) * piece)], spread_send)
         sent(remote_sum.at[:, pl.ds(offsets[RAW], order - offsets[RAW])], sum_send)

time: 74.9 us -> 72.1 us (0.963)
  Pallas kernels: 73.5 us -> 70.1 us
    pallas_call x1, Pallas kernels: 73.5 us -> 70.1 us  [line_call(): pl.pallas_call(functools.partial(line_kernel, n_alpha, n_beta, rounds, he...]
where the time goes in v4:
time: 72.1 us; the launch traced here: 71.4 us
  Pallas kernels  70.1 us (97%)
  local copies, waits for them, and re-layouts  1.32 us (2%)
    pallas_call x1, Pallas kernels, line_call(): pl.pallas_call(functools.partial(line_kernel, n_alpha, n_beta, rounds, he...  70.1 us

profile of v4, /device:TPU:0, one launch (start us, length us, event | category | flops | bytes accessed | tf_op | source)
XLA Modules:
  0.0 71.4 jit_solution(828127322505170246)
XLA Ops:
  0.0 70.1 %shard_map.55 = f32[512,1024]{1,0:T(8,128)S(1)} custom-call(s32[3,8,8]{2,1,0:T(8,128)} %bitcast.3, s32[8,8]{1,0:T(8,128)} %counts_hbm.1, bf16[8,256,256]{2,1,0:T(8,128)(2,1)} %coupling_hbm.1, bf16[2,256,1024]{2,1,0:T(8,128)(2,1)} %bitcast.2, bf16[4,1024,1024]{2,1,0:T(8,128)(2,1)} %b_hbm.1), custom_call_target="tpu_custom_call" | custom-call | tf_op jit(solution)/shard_map/pallas_call | solution.py:581
  70.1 1.3 %copy.7 = f32[512,1024]{1,0:T(8,128)} copy(f32[512,1024]{1,0:T(8,128)S(1)} %shard_map.55) | data formatting | bytes 4194304

commit v5 on v4

--- a/solution.py
+++ b/solution.py
@@ -11,8 +11,8 @@
 WIDTHS = (1, 2, 2, 2, 1)
 TILE = 256
 AHEAD = 1
-SHARES = (1, 1, 1, 1, 1, 1, 1, 1)
-PIECES = 4
+SHARES = (2, 2, 2, 2, 2, 2, 2, 1, 1)
+PIECES = 8
 LAG = 2
 RAW = 2
 FIRST = 4
@@ -198,7 +198,7 @@
 
 def line_kernel(
     n_alpha, n_beta, rounds, heights,
-    exc_hbm, counts_hbm, coupling_hbm, c_hbm, b_hbm, out_ref,
+    exc_hbm, counts_hbm, coupling_hbm, c_hbm, b_hbm, out_ref, last_weights, last_gathered,
     exc_ref, counts_ref, coupling_ref, weights, tiles, blocks, outer_tiles, partial, remote_sum, held, gathered,
     in_sem, raw_send, raw_recv, sum_send, sum_recv, tile_send, tile_recv, spread_send, spread_recv, spread_last,
     send_sem, recv_sem,
@@ -265,8 +265,8 @@
         source = c_hbm.at[:, rows_of(c)] if kind < 2 else blocks.at[plane, :, rows_of(c)]
         return remote(source, blocks.at[plane, :, rows_of(c)], raw_send.at[kind], raw_recv.at[plane, c], device)
 
-    def sum_copy(c):
-        here = remote_sum.at[:, rows_of(c)]
+    def sum_copy(c, first=0, width=columns):
+        here = remote_sum.at[:, rows_of(c), pl.ds(first, width)]
         return remote(here, here, sum_send, sum_recv.at[c], near)
 
     piece = 2 * b_hbm.shape[1] // n_alpha
@@ -326,16 +326,16 @@
             for block in range(n_blocks):
                 keep = jnp.where(live & (target == block), 1.0, 0.0).astype(jnp.float32)
                 value = (matrix.astype(jnp.float32) * keep).astype(jnp.bfloat16)
-                for half in range(order // LANES):
-                    weights[half, pl.ds(block * order, order), pl.ds(slot * LANES, LANES)] = value[
-                        :, half * LANES : (half + 1) * LANES
-                    ]
+                at = (pl.ds(block * order, order), pl.ds(slot * LANES, LANES))
+                for half in range(order // LANES - 1):
+                    weights[(half, *at)] = value[:, half * LANES : (half + 1) * LANES]
+                last_weights[at] = value[:, order - LANES :]
         return picked
 
-    def product(first, count, planes, tile, store, before=False):
+    def product(first, count, planes, tile, store, before=False, start=0, stop=columns):
         at_rows = pl.ds(offsets[first], sum(heights[first : first + count]))
 
-        @pl.loop(0, columns // TILE)
+        @pl.loop(start // TILE, stop // TILE)
         def _(n):
             at = pl.ds(pl.multiple_of(n * TILE, TILE), TILE)
             value = None
@@ -373,9 +373,11 @@
     def finish(c, picked):
         held_arrive(c, rounds)
         half, within = offsets[c] // LANES, offsets[c] % LANES
+        final = half == order // LANES - 1
+        panel = last_gathered if final else gathered.at[half]
         for slot in range(n_alpha):
-            gathered[half, pl.ds(slot * LANES + within, heights[c])] = held[c][slot, picked[slot]]
-        if within + heights[c] == LANES:
+            panel[pl.ds(slot * LANES + within, heights[c])] = held[c][slot, picked[slot]]
+        if within + heights[c] == LANES and not final:
             @pl.loop(0, columns // TILE)
             def _(n):
                 at = pl.ds(pl.multiple_of(n * TILE, TILE), TILE)
@@ -402,8 +404,8 @@
         advance(rounds, chunks - 1 - 2 * LAG, picked)
         for group in range(rounds - 1):
             advance(group, chunks - 1, picked)
-        advance(rounds - 1, chunks - 1 - LAG, picked)
-        advance(rounds, chunks - 1 - LAG, picked)
+        advance(rounds - 1, chunks - 2 - LAG, picked)
+        advance(rounds, chunks - 2 - LAG, picked)
         advance(rounds - 1, chunks - 1, picked)
         advance(rounds, chunks - 1, picked)
         for c in range(chunks):
@@ -491,9 +493,14 @@
                 if SECOND <= c + 1 < chunks:
                     own_facing(c + 1)
 
-        def tile_own(q):
-            tile_copy(q).wait_recv()
-            spread(tile_spread, q, 0)
+        def tile_own(pair):
+            for q in (2 * pair, 2 * pair + 1):
+                tile_copy(q).wait_recv()
+                spread(tile_spread, q, 0)
+
+        def tile_pass(pair, group):
+            for q in (2 * pair, 2 * pair + 1):
+                tile_relay(q, group)
 
         def finish_held(c):
             product(c, 1, (outer, beyond), own_tile, store_held(c), before=True)
@@ -505,7 +512,7 @@
 
         def hold(c, lag):
             if c >= FIRST and c % 2 == 0:
-                product(c, 2, (inner, across), own_tile, store_partial)
+                product(c, min(2, chunks - c), (inner, across), own_tile, store_partial)
             finish_held(c)
             follow(c, lag, picked)
 
@@ -522,26 +529,26 @@
         pass_on(0)
         own_facing(4)
         own_facing(5)
-        tile_relay(0, 0)
+        tile_pass(0, 0)
         tile_own(2)
-        tile_relay(1, 0)
+        tile_pass(1, 0)
         prepare(2)
         tile_own(3)
-        tile_relay(0, 1)
+        tile_pass(0, 1)
         send_beyond(0)
         own_near(4)
         own_near(5)
-        tile_relay(2, 0)
+        tile_pass(2, 0)
         pass_on(1)
-        tile_relay(1, 1)
+        tile_pass(1, 1)
         product(0, 1, (outer, beyond), own_tile, store_held(0), before=True)
-        tile_relay(3, 0)
+        tile_pass(3, 0)
         pass_on(2)
         spread(held_spread, 0, 0)
-        tile_relay(2, 1)
+        tile_pass(2, 1)
         pass_on(3)
         send_beyond(1)
-        tile_relay(3, 1)
+        tile_pass(3, 1)
         hold(1, 1)
         pass_on(4)
         here = outer_tiles.at[pl.ds(0, n_chips * piece)]
@@ -550,8 +557,9 @@
             if c >= FIRST:
                 raw(c, across, 1, facing).wait_recv()
             raw(c, beyond, 2, facing).wait_recv()
-            product(c, 1, (across, beyond), far_tile, store_sum)
-            sum_copy(c).start()
+            for first in range(0, columns, columns // 2):
+                product(c, 1, (across, beyond), far_tile, store_sum, start=first, stop=first + columns // 2)
+                sum_copy(c, first, columns // 2).start()
             if SECOND <= c + 1 < chunks:
                 own_near(c + 1)
             pass_on(c + 3)
@@ -578,23 +586,27 @@
     rounds = (n_alpha // 2).bit_length() - 1
     hbm = pl.BlockSpec(memory_space=pl.ANY)
     dma = pltpu.SemaphoreType.DMA
-    return pl.pallas_call(
+    total, last_weights, last_gathered = pl.pallas_call(
         functools.partial(line_kernel, n_alpha, n_beta, rounds, heights),
-        out_shape=pltpu.VMEM((rows, columns), jnp.float32),
+        out_shape=[
+            pltpu.VMEM((rows, columns), jnp.float32),
+            pltpu.VMEM((rows, n_alpha * LANES), jnp.bfloat16),
+            pltpu.VMEM((n_alpha * LANES, columns), jnp.bfloat16),
+        ],
         in_specs=[hbm] * 5,
-        out_specs=pl.BlockSpec(memory_space=pltpu.VMEM),
+        out_specs=[pl.BlockSpec(memory_space=pltpu.VMEM)] * 3,
         scratch_shapes=[
             pltpu.SMEM((3, n_alpha, n_alpha), jnp.int32),
             pltpu.SMEM((n_alpha, n_alpha), jnp.int32),
             pltpu.VMEM(couplings.shape, jnp.bfloat16),
-            pltpu.VMEM((order // LANES, rows, n_alpha * LANES), jnp.bfloat16),
+            pltpu.VMEM((order // LANES - 1, rows, n_alpha * LANES), jnp.bfloat16),
             pltpu.VMEM(beta_tiles.shape, jnp.bfloat16),
             pltpu.VMEM((n_beta, n_blocks, order, columns), jnp.bfloat16),
             pltpu.VMEM((2 * columns, columns), jnp.bfloat16),
             pltpu.VMEM((n_blocks, order, columns), jnp.float32),
             pltpu.VMEM((n_blocks, order, columns), jnp.bfloat16),
             [pltpu.VMEM((n_alpha, n_blocks, height, columns), jnp.bfloat16) for height in heights],
-            pltpu.VMEM((order // LANES, n_alpha * LANES, columns), jnp.bfloat16),
+            pltpu.VMEM((order // LANES - 1, n_alpha * LANES, columns), jnp.bfloat16),
             dma((5,)),
             dma((4,)),
             dma((n_beta, chunks)),
@@ -618,6 +630,7 @@
         coefficients.reshape(n_blocks, order, columns),
         beta_tiles,
     )
+    return total + jnp.dot(last_weights, last_gathered, preferred_element_type=jnp.float32)
 
 
 def solution(mesh):

time: 72.1 us -> 71.1 us (0.986)
  matrix products: 0 us -> 2.04 us
  local copies, waits for them, and re-layouts: 1.32 us -> 0 us
  Pallas kernels: 70.1 us -> 69 us
    dot_general x0 -> x1, matrix products: none -> 2.04 us  [line_call(): jnp.dot(last_weights, last_gathered, preferred_element_type=jnp.float32)]
    unnamed x1 -> x0, local copies, waits for them, and re-layouts: 1.32 us -> none
    pallas_call x1, Pallas kernels: 70.1 us -> 69 us  [line_call(): pl.pallas_call(functools.partial(line_kernel, n_alpha, n_beta, rounds, he...]
where the time goes in v5:
time: 71.1 us; the launch traced here: 71 us
  Pallas kernels  69 us (97%)
  matrix products  2.04 us (3%)
    pallas_call x1, Pallas kernels, line_call(): pl.pallas_call(functools.partial(line_kernel, n_alpha, n_beta, rounds, he...  69 us
    dot_general x1, matrix products, line_call(): jnp.dot(last_weights, last_gathered, preferred_element_type=jnp.float32)  2.04 us

profile of v5, /device:TPU:0, one launch (start us, length us, event | category | flops | bytes accessed | tf_op | source)
XLA Modules:
  0.0 71.0 jit_solution(10232168334180406962)
XLA Ops:
  0.0 69.0 %shard_map.55 = (f32[512,1024]{1,0:T(8,128)S(1)}, bf16[512,512]{1,0:T(8,128)(2,1)S(1)}, bf16[512,1024]{1,0:T(8,128)(2,1)S(1)}) custom-call(s32[3,8,8]{2,1,0:T(8,128)} %bitcast.5, s32[8,8]{1,0:T(8,128)} %counts_hbm.1, bf16[8,256,256]{2,1,0:T(8,128)(2,1)} %coupling_hbm.1, bf16[2,256,1024]{2,1,0:T(8,128)(2,1)} %bitcast.4, bf16[4,1024,1024]{2,1,0:T(8,128)(2,1)} %b_hbm.1), custom_call_target="tpu_custom_call" | custom-call | tf_op jit(solution)/shard_map/pallas_call | solution.py:589
  69.0 2.0 %convolution_add_fusion = f32[512,1024]{1,0:T(8,128)} fusion(f32[512,1024]{1,0:T(8,128)S(1)} %get-tuple-element.8, bf16[512,512]{1,0:T(8,128)(2,1)S(1)} %get-tuple-element.9, bf16[512,1024]{1,0:T(8,128)(2,1)S(1)} %get-tuple-element.10), kind=kOutput, calls=%fused_computation | convolution fusion | flops 537395200 | bytes 5767168 | tf_op jit(solution)/shard_map/dot_general | solution.py:633
